TPU v7x, 256 devices: a whole 4x4x8 slice. The times are simulated.
256 devices in a mesh: dp: 32 (over y, x, z_lo), cam: 8 (over z_hi, core).
Axes of the slice: x: 4, y: 4, z: 8 (z_hi: 4, z_lo: 2; z = z_hi * 2 + z_lo), core: 2. Of those that a mesh axis runs over, the one named last changes fastest.
Arguments:
- grad_out: bfloat16 [32768, 3072], P(('dp', 'cam')), may hold values from -6 to 6
- query_act: bfloat16 [32768, 2048], P(('dp', 'cam')), may hold values from -13 to 13
- key_act: bfloat16 [32768, 2048], P(('dp', 'cam')), may hold values from -13 to 13
- value_act: bfloat16 [32768, 2048], P(('dp', 'cam')), may hold values from -6 to 6
- out_proj: bfloat16 [3072, 2048], P('dp'), may hold values from -0.125 to 0.125
- view_counts: int32 [32, 4], P('dp'), may hold values from 1 to 12, 16 in all within a row
- view_slots: int32 [32, 16], P('dp'), may hold values from 0 to 15, each once within a row
Outputs:
- grad_query: bfloat16 [32768, 2048], P(('dp', 'cam'))
- grad_key: bfloat16 [32768, 2048], P(('dp', 'cam'))
- grad_value: bfloat16 [32768, 2048], P(('dp', 'cam'))
- grad_proj: float32 [3072, 2048], P('dp')
Inputs may be any that keep to these rules, and one draw needn't show every extreme that they name: `view_counts`: in each group the 4 counts sum to 16, and the largest is exactly 12. `view_slots`: each row is a permutation of the group's 16 slots.
All inputs are finite; a program needn't handle non-finite values.
Results may differ from a plain program's by a relative error of at most 0.0096.
Values may be sent and summed in bfloat16 or wider, within the bound.
A program may use at most 64 MiB of HBM per device.

v0:
```python
import math
import jax
import jax.numpy as jnp
from jax import lax
from jax.sharding import PartitionSpec as P

HEAD_DIM = 128
VIEW_TOK = 64


def token_objects(counts, slots, view_tokens):
    count_ends = jnp.cumsum(counts)
    view_order = jnp.arange(slots.shape[0], dtype=jnp.int32)
    view_object = jnp.sum((view_order[:, None] >= count_ends[None, :]).astype(jnp.int32), axis=1)
    placed = slots[:, None] == view_order[None, :]
    slot_object = jnp.sum(jnp.where(placed, view_object[:, None], 0), axis=0)
    return jnp.repeat(slot_object, view_tokens)


def head_attention(query_heads, key_heads, value_heads, grad_heads, same_object, head_dim):
    group_tokens, proj_width = query_heads.shape
    head_count = proj_width // head_dim
    score_scale = 1.0 / math.sqrt(head_dim)

    def one_head(head_index):
        first_col = head_index * head_dim
        query_one = lax.dynamic_slice_in_dim(query_heads, first_col, head_dim, 1)
        key_one = lax.dynamic_slice_in_dim(key_heads, first_col, head_dim, 1)
        value_one = lax.dynamic_slice_in_dim(value_heads, first_col, head_dim, 1)
        grad_one = lax.dynamic_slice_in_dim(grad_heads, first_col, head_dim, 1)
        scores = (
            lax.dot_general(
                query_one, key_one, (((1,), (1,)), ((), ())), preferred_element_type=jnp.float32
            )
            * score_scale
        )
        scores = jnp.where(same_object, scores, -jnp.inf)
        row_max = jnp.max(scores, axis=1, keepdims=True)
        exp_scores = jnp.exp(scores - row_max)
        probs = exp_scores / jnp.sum(exp_scores, axis=1, keepdims=True)
        probs_bf16 = probs.astype(jnp.bfloat16)
        attended_f32 = jnp.dot(probs_bf16, value_one, preferred_element_type=jnp.float32)
        row_delta = jnp.sum(grad_one.astype(jnp.float32) * attended_f32, axis=1)
        grad_probs = lax.dot_general(
            grad_one, value_one, (((1,), (1,)), ((), ())), preferred_element_type=jnp.float32
        )
        grad_scores = (probs * (grad_probs - row_delta[:, None])).astype(jnp.bfloat16)
        grad_query = jnp.dot(grad_scores, key_one, preferred_element_type=jnp.float32) * score_scale
        grad_key = (
            lax.dot_general(
                grad_scores, query_one, (((0,), (0,)), ((), ())), preferred_element_type=jnp.float32
            )
            * score_scale
        )
        grad_value = lax.dot_general(
            probs_bf16, grad_one, (((0,), (0,)), ((), ())), preferred_element_type=jnp.float32
        )
        return (
            attended_f32.astype(jnp.bfloat16),
            grad_query.astype(jnp.bfloat16),
            grad_key.astype(jnp.bfloat16),
            grad_value.astype(jnp.bfloat16),
        )

    stacked = lax.map(one_head, jnp.arange(head_count, dtype=jnp.int32))

    def flatten(per_head):
        return jnp.transpose(per_head, (1, 0, 2)).reshape(group_tokens, proj_width)

    return tuple((flatten(item) for item in stacked))


def local(grad_out, query_act, key_act, value_act, out_proj, view_counts, view_slots):
    objects = token_objects(view_counts[0], view_slots[0], VIEW_TOK)
    same_object = objects[:, None] == objects[None, :]
    whole_out = lax.all_gather(grad_out, "cam", axis=0, tiled=True)
    columns = grad_out
    grad_attn = jnp.dot(
        columns,
        lax.all_gather(out_proj, "dp", axis=0, tiled=True),
        preferred_element_type=jnp.float32,
    ).astype(jnp.bfloat16)
    query_heads, key_heads, value_heads, grad_heads = (
        lax.all_to_all(query_act, "cam", split_axis=1, concat_axis=0, tiled=True),
        lax.all_to_all(key_act, "cam", split_axis=1, concat_axis=0, tiled=True),
        lax.all_to_all(value_act, "cam", split_axis=1, concat_axis=0, tiled=True),
        lax.all_to_all(grad_attn, "cam", split_axis=1, concat_axis=0, tiled=True),
    )
    attended, grad_query, grad_key, grad_value = head_attention(
        query_heads, key_heads, value_heads, grad_heads, same_object, HEAD_DIM
    )
    columns = whole_out
    partial_rows = lax.psum_scatter(
        lax.dot_general(
            columns, attended, (((0,), (0,)), ((), ())), preferred_element_type=jnp.float32
        ),
        "dp",
        scatter_dimension=0,
        tiled=True,
    )
    grad_proj = lax.all_gather(partial_rows, "cam", axis=1, tiled=True)
    grad_query, grad_key, grad_value = (
        lax.all_to_all(grad_query, "cam", split_axis=0, concat_axis=1, tiled=True),
        lax.all_to_all(grad_key, "cam", split_axis=0, concat_axis=1, tiled=True),
        lax.all_to_all(grad_value, "cam", split_axis=0, concat_axis=1, tiled=True),
    )
    return (grad_query, grad_key, grad_value, grad_proj)


def solution(mesh):
    in_specs = (
        P(("dp", "cam"), None),
        P(("dp", "cam"), None),
        P(("dp", "cam"), None),
        P(("dp", "cam"), None),
        P("dp", None),
        P("dp", None),
        P("dp", None),
    )
    out_specs = (
        P(("dp", "cam"), None),
        P(("dp", "cam"), None),
        P(("dp", "cam"), None),
        P("dp", None),
    )
    return jax.shard_map(local, mesh=mesh, in_specs=in_specs, out_specs=out_specs, check_vma=False)
```

profile of v0, /device:TPU:1, one launch (start us, length us, event | category | flops | bytes accessed | tf_op | source)
XLA Modules:
  0.0 621.5 jit_solution(6285375771550483284)
XLA Ops:
  10.5 10.0 %all-to-all-start = ((bf16[128,8,256]{2,0,1:T(8,128)(2,1)}), bf16[128,8,256]{2,0,1:T(8,128)(2,1)S(1)}, u32[]{:S(2)}, u32[]{:S(2)}) async-start(bf16[128,8,256]{2,0,1:T(8,128)(2,1)} %bitcast.86), calls=%async_computation | async-start | bytes 1048576 | tf_op jit(solution)/shard_map/all_to_all | solution.py:84
  22.4 17.7 %all-to-all-done = bf16[128,8,256]{2,0,1:T(8,128)(2,1)S(1)} async-done(((bf16[128,8,256]{2,0,1:T(8,128)(2,1)}), bf16[128,8,256]{2,0,1:T(8,128)(2,1)S(1)}, u32[]{:S(2)}, u32[]{:S(2)}) %all-to-all-start) | async-done | bytes 524320 | tf_op jit(solution)/shard_map/all_to_all | solution.py:84
  40.1 5.0 all-to-all-start.1
  45.9 22.4 %all-to-all-done.1 = bf16[128,8,256]{2,0,1:T(8,128)(2,1)S(1)} async-done(((bf16[128,8,256]{2,0,1:T(8,128)(2,1)}), bf16[128,8,256]{2,0,1:T(8,128)(2,1)S(1)}, u32[]{:S(2)}, u32[]{:S(2)}) %all-to-all-start.1) | async-done | bytes 524320 | tf_op jit(solution)/shard_map/all_to_all | solution.py:85
  68.3 4.0 all-to-all-start.2
  72.3 250.5 %all-gather.3.cloned.1.call-done = bf16[3072,2048]{1,0:T(8,128)(2,1)} async-done(((bf16[96,2048]{1,0:T(8,128)(2,1)}), bf16[3072,2048]{1,0:T(8,128)(2,1)}) %all-gather.3.cloned.1.call-update) | async-done | bytes 12582928 | tf_op jit(solution)/shard_map/all_gather | solution.py:80
  322.8 6.4 %convolution_convert_fusion.1 = bf16[128,2048]{1,0:T(8,128)(2,1)S(1)} fusion(bf16[128,3072]{1,0:T(8,128)(2,1)S(1)} %copy-done.2, bf16[3072,2048]{1,0:T(8,128)(2,1)} %all-gather.3.cloned.1.call-done), kind=kOutput, calls=%fused_computation.37 | convolution fusion | flops 1610874880 | bytes 13893632 | tf_op jit(solution)/shard_map/dot_general | solution.py:78
  330.0 6.9 %all-to-all-start.3 = ((bf16[128,8,256]{2,0,1:T(8,128)(2,1)}), bf16[128,8,256]{2,0,1:T(8,128)(2,1)S(1)}, u32[]{:S(2)}, u32[]{:S(2)}) async-start(bf16[128,8,256]{2,0,1:T(8,128)(2,1)} %bitcast.83), calls=%async_computation.3 | async-start | bytes 1048576 | tf_op jit(solution)/shard_map/all_to_all | solution.py:87
  337.5 35.0 %all-to-all-done.3 = bf16[128,8,256]{2,0,1:T(8,128)(2,1)S(1)} async-done(((bf16[128,8,256]{2,0,1:T(8,128)(2,1)}), bf16[128,8,256]{2,0,1:T(8,128)(2,1)S(1)}, u32[]{:S(2)}, u32[]{:S(2)}) %all-to-all-start.3) | async-done | bytes 524320 | tf_op jit(solution)/shard_map/all_to_all | solution.py:87
  372.5 30.3 %while.17 = (s32[]{:T(128)}, bf16[2,1024,128]{1,2,0:T(8,128)(2,1)}, bf16[2,1024,128]{2,1,0:T(8,128)(2,1)S(1)}, bf16[2,1024,128]{2,1,0:T(8,128)(2,1)}, bf16[2,102...) while((s32[]{:T(128)}, bf16[2,1024,128]{1,2,0:T(8,128)(2,1)}, ...), condition=%wide.region_7.8_spmd.clone, body=%wide.region_3.7_spmd.clone.sunk | while | flops 1631712256 | bytes 87341000 | solution.py:65
  376.9 1.9 copy-done
  380.4 3.0 multiply_convert_fusion.2
  392.0 1.9 copy-done
  395.5 3.0 multiply_convert_fusion.2
  403.8 4.8 convolution_bitcast_fusion
  408.6 2.4 copy.89
  413.3 3.7 all-to-all-start.4
  418.2 18.1 %all-to-all-done.4 = bf16[8,128,256]{1,2,0:T(8,128)(2,1)S(1)} async-done(((bf16[8,128,256]{1,2,0:T(8,128)(2,1)}), bf16[8,128,256]{1,2,0:T(8,128)(2,1)S(1)}, u32[]{:S(2)}, u32[]{:S(2)}) %all-to-all-start.4) | async-done | bytes 524320 | tf_op jit(solution)/shard_map/all_to_all | solution.py:103
  436.3 4.9 all-to-all-start.5
  442.4 20.0 %all-to-all-done.5 = bf16[8,128,256]{1,2,0:T(8,128)(2,1)S(1)} async-done(((bf16[8,128,256]{1,2,0:T(8,128)(2,1)}), bf16[8,128,256]{1,2,0:T(8,128)(2,1)S(1)}, u32[]{:S(2)}, u32[]{:S(2)}) %all-to-all-start.5) | async-done | bytes 524320 | tf_op jit(solution)/shard_map/all_to_all | solution.py:104
  462.4 4.4 all-to-all-start.6
  468.7 20.9 %all-to-all-done.6 = bf16[8,128,256]{1,2,0:T(8,128)(2,1)S(1)} async-done(((bf16[8,128,256]{1,2,0:T(8,128)(2,1)}), bf16[8,128,256]{1,2,0:T(8,128)(2,1)S(1)}, u32[]{:S(2)}, u32[]{:S(2)}) %all-to-all-start.6) | async-done | bytes 524320 | tf_op jit(solution)/shard_map/all_to_all | solution.py:105
  490.6 81.5 %reduce-scatter.4.cloned.1.call-done = f32[96,256]{1,0:T(8,128)} async-done(((f32[3072,256]{1,0:T(8,128)}), f32[96,256]{1,0:T(8,128)}) %reduce-scatter.4.cloned.1.call-update) | async-done | bytes 98320
  573.1 40.6 %all_gather.11 = f32[96,2048]{0,1:T(8,128)S(1)} all-gather(f32[96,256]{0,1:T(8,128)S(1)} %copy.90), channel_id=1, replica_groups=mesh['dp'=32,'cam'=8] {'cam'}, dimensions={1}, use_global_device_ids=true | all-gather | bytes 884736 | tf_op jit(solution)/shard_map/all_gather | solution.py:101
  (102 shorter events, 37.3 us)
Async XLA Ops:
  7.2 315.7 %copy-start.2 = (bf16[128,3072]{1,0:T(8,128)(2,1)S(1)}, bf16[128,3072]{1,0:T(8,128)(2,1)}, u32[]{:S(2)}) copy-start(bf16[128,3072]{1,0:T(8,128)(2,1)} %param.9) | copy-start | bytes 2359300
  7.2 37.9 %copy-start.3 = (bf16[128,2048]{1,0:T(8,128)(2,1)S(1)}, bf16[128,2048]{1,0:T(8,128)(2,1)}, u32[]{:S(2)}) copy-start(bf16[128,2048]{1,0:T(8,128)(2,1)} %param.12) | copy-start | bytes 1572868
  7.2 315.6 %all-gather.3.cloned.1.call-start = ((), (), s32[]{:S(2)}) async-start(), calls=%async_computation.8 | async-start | bytes 12976128 | tf_op jit(solution)/shard_map/all_gather | solution.py:80
  7.9 395.9 %all-gather.5.cloned.1.call-start = ((), (), s32[]{:S(2)}) async-start(), calls=%async_computation.9 | async-start | bytes 7077888 | tf_op jit(solution)/shard_map/all_gather | solution.py:76
  10.5 29.5 %all-to-all-start = ((bf16[128,8,256]{2,0,1:T(8,128)(2,1)}), bf16[128,8,256]{2,0,1:T(8,128)(2,1)S(1)}, u32[]{:S(2)}, u32[]{:S(2)}) async-start(bf16[128,8,256]{2,0,1:T(8,128)(2,1)} %bitcast.86), calls=%async_computation | async-start | bytes 1048576 | tf_op jit(solution)/shard_map/all_to_all | solution.py:84
  40.1 28.2 %all-to-all-start.1 = ((bf16[128,8,256]{2,0,1:T(8,128)(2,1)}), bf16[128,8,256]{2,0,1:T(8,128)(2,1)S(1)}, u32[]{:S(2)}, u32[]{:S(2)}) async-start(bf16[128,8,256]{2,0,1:T(8,128)(2,1)} %bitcast.85), calls=%async_computation.1 | async-start | bytes 1048576 | tf_op jit(solution)/shard_map/all_to_all | solution.py:85
  68.3 261.7 %all-to-all-start.2 = ((bf16[128,8,256]{2,0,1:T(8,128)(2,1)}), bf16[128,8,256]{2,0,1:T(8,128)(2,1)S(1)}, u32[]{:S(2)}, u32[]{:S(2)}) async-start(bf16[128,8,256]{2,0,1:T(8,128)(2,1)} %bitcast.84), calls=%async_computation.2 | async-start | bytes 1048576 | tf_op jit(solution)/shard_map/all_to_all | solution.py:86
  72.3 264.6 %copy-start.13 = (s32[1,4]{1,0:T(1,128)S(1)}, s32[1,4]{1,0:T(1,128)}, u32[]{:S(2)}) copy-start(s32[1,4]{1,0:T(1,128)} %param.14) | copy-start | bytes 52
  72.3 264.9 %copy-start.14 = (s32[1,16]{1,0:T(1,128)S(1)}, s32[1,16]{1,0:T(1,128)}, u32[]{:S(2)}) copy-start(s32[1,16]{1,0:T(1,128)} %param.15) | copy-start | bytes 196
  330.0 42.4 %all-to-all-start.3 = ((bf16[128,8,256]{2,0,1:T(8,128)(2,1)}), bf16[128,8,256]{2,0,1:T(8,128)(2,1)S(1)}, u32[]{:S(2)}, u32[]{:S(2)}) async-start(bf16[128,8,256]{2,0,1:T(8,128)(2,1)} %bitcast.83), calls=%async_computation.3 | async-start | bytes 1048576 | tf_op jit(solution)/shard_map/all_to_all | solution.py:87
  336.9 235.2 %reduce-scatter.4.cloned.1.call-start = ((), (), s32[]{:S(2)}) async-start(), calls=%async_computation.10 | async-start | bytes 3244032
  372.5 3.0 copy-start.4
  380.3 3.1 copy-start.7
  380.4 3.9 copy-start.5
  383.4 2.5 copy-start.10
  387.6 3.0 copy-start.4
  395.4 3.2 copy-start.7
  395.5 3.9 copy-start.5
  398.5 2.5 copy-start.10
  410.9 6.1 copy-start.9
  411.0 30.2 %copy-start.12 = (bf16[2,1024,128]{2,1,0:T(8,128)(2,1)S(1)}, bf16[2,1024,128]{2,1,0:T(8,128)(2,1)}, u32[]{:S(2)}) copy-start(bf16[2,1024,128]{2,1,0:T(8,128)(2,1)} %get-tuple-element.66) | copy-start | bytes 1572868
  413.3 23.0 %all-to-all-start.4 = ((bf16[8,128,256]{1,2,0:T(8,128)(2,1)}), bf16[8,128,256]{1,2,0:T(8,128)(2,1)S(1)}, u32[]{:S(2)}, u32[]{:S(2)}) async-start(bf16[8,128,256]{1,2,0:T(8,128)(2,1)} %copy.79), calls=%async_computation.4 | async-start | bytes 1048576 | tf_op jit(solution)/shard_map/all_to_all | solution.py:103
  436.3 26.1 %all-to-all-start.5 = ((bf16[8,128,256]{1,2,0:T(8,128)(2,1)}), bf16[8,128,256]{1,2,0:T(8,128)(2,1)S(1)}, u32[]{:S(2)}, u32[]{:S(2)}) async-start(bf16[8,128,256]{1,2,0:T(8,128)(2,1)} %copy.81), calls=%async_computation.5 | async-start | bytes 1048576 | tf_op jit(solution)/shard_map/all_to_all | solution.py:104
  462.4 27.3 %all-to-all-start.6 = ((bf16[8,128,256]{1,2,0:T(8,128)(2,1)}), bf16[8,128,256]{1,2,0:T(8,128)(2,1)S(1)}, u32[]{:S(2)}, u32[]{:S(2)}) async-start(bf16[8,128,256]{1,2,0:T(8,128)(2,1)} %copy.83), calls=%async_computation.6 | async-start | bytes 1048576 | tf_op jit(solution)/shard_map/all_to_all | solution.py:105
  (9 other events, 13.2 us)
Sparse Core Ops, SparseCore 0:
  9.8 312.9 all-gather.2
  324.6 79.1 all-gather.4
  411.1 161.0 reduce-scatter.3
where the time goes:
time: 622 us; the launch traced here: 621 us
  waiting for transfers between devices  469 us (75%)
  blocking collectives  40.6 us (7%)
  starting transfers between devices  38.9 us (6%)
  local copies, waits for them, and re-layouts  26.6 us (4%)
  matrix products  26.2 us (4%)
  between operations  13.9 us (2%)
    all_gather x1, waiting for transfers between devices, local(): lax.all_gather(out_proj, 'dp', axis=0, tiled=True)  250 us
    unnamed x4, waiting for transfers between devices  82.9 us
    all_gather x1, blocking collectives, local(): grad_proj = lax.all_gather(partial_rows, 'cam', axis=1, tiled=True)  40.6 us
    all_to_all x1, waiting for transfers between devices, local(): lax.all_to_all(grad_attn, 'cam', split_axis=1, concat_axis=0, tiled=True)  35 us
    all_to_all x1, waiting for transfers between devices, local(): lax.all_to_all(key_act, 'cam', split_axis=1, concat_axis=0, tiled=True)  22.4 us
    all_to_all x1, waiting for transfers between devices, local(): lax.all_to_all(grad_value, 'cam', split_axis=0, concat_axis=1, tiled=True)  20.9 us
    all_to_all x1, waiting for transfers between devices, local(): lax.all_to_all(grad_key, 'cam', split_axis=0, concat_axis=1, tiled=True)  20 us
    all_to_all x1, waiting for transfers between devices, local(): lax.all_to_all(grad_query, 'cam', split_axis=0, concat_axis=1, tiled=True)  18.1 us
  transfers between devices with their start and end apart: 10, of which 9 were waited for; matrix products, arithmetic and copies ran while one was open for 7% of the time, Pallas kernels for 0%

commit v1 on v0

--- a/solution.py
+++ b/solution.py
@@ -75,10 +75,11 @@
     same_object = objects[:, None] == objects[None, :]
     whole_out = lax.all_gather(grad_out, "cam", axis=0, tiled=True)
     columns = grad_out
+    sample_assign = lambda inp: jnp.concatenate(
+        jax.lax.all_to_all(jnp.stack(jax.lax.axis_size("dp") * [inp], 0), "dp", 0, 0), axis=0
+    )
     grad_attn = jnp.dot(
-        columns,
-        lax.all_gather(out_proj, "dp", axis=0, tiled=True),
-        preferred_element_type=jnp.float32,
+        columns, sample_assign(out_proj), preferred_element_type=jnp.float32
     ).astype(jnp.bfloat16)
     query_heads, key_heads, value_heads, grad_heads = (
         lax.all_to_all(query_act, "cam", split_axis=1, concat_axis=0, tiled=True),

time: 622 us -> 596 us (0.958)
  waiting for transfers between devices: 469 us -> 389 us
  starting transfers between devices: 38.9 us -> 64.4 us
  blocking collectives: 40.6 us -> 61.3 us
    all_gather x1 -> x0, waiting for transfers between devices: 250 us -> none  [local(): lax.all_gather(out_proj, 'dp', axis=0, tiled=True)]
    all_to_all x1, waiting for transfers between devices: 22.4 us -> 199 us  [local(): jax.lax.all_to_all(jnp.stack(jax.lax.axis_size('dp') * [inp], 0), 'dp', 0...]
    unnamed x4 -> x3, waiting for transfers between devices: 82.9 us -> 107 us
    all_to_all x1, waiting for transfers between devices: 35 us -> 12.9 us  [local(): lax.all_to_all(grad_attn, 'cam', split_axis=1, concat_axis=0, tiled=True)]
    all_to_all x0 -> x1, blocking collectives: none -> 22 us  [local(): lax.all_to_all(key_act, 'cam', split_axis=1, concat_axis=0, tiled=True)]
    all_to_all x1, starting transfers between devices: 4.05 us -> 24 us  [local(): lax.all_to_all(value_act, 'cam', split_axis=1, concat_axis=0, tiled=True)]
    all_to_all x1, waiting for transfers between devices: 0.01 us -> 8.14 us  [local(): lax.all_to_all(value_act, 'cam', split_axis=1, concat_axis=0, tiled=True)]
  transfers between devices with their start and end apart: 10 -> 9, of which waited for: 9 -> 8; matrix products, arithmetic and copies ran while one was open for 7% -> 7% of each run, Pallas kernels for 0% -> 0%
where the time goes in v1:
time: 596 us; the launch traced here: 595 us
  waiting for transfers between devices  389 us (65%)
  starting transfers between devices  64.4 us (11%)
  blocking collectives  61.3 us (10%)
  local copies, waits for them, and re-layouts  32.2 us (5%)
  matrix products  27.1 us (5%)
  between operations  14.2 us (2%)
    all_to_all x1, waiting for transfers between devices, local(): jax.lax.all_to_all(jnp.stack(jax.lax.axis_size('dp') * [inp], 0), 'dp', 0...  199 us
    unnamed x3, waiting for transfers between devices  107 us
    all_gather x1, blocking collectives, local(): grad_proj = lax.all_gather(partial_rows, 'cam', axis=1, tiled=True)  39.3 us
    all_to_all x1, starting transfers between devices, local(): lax.all_to_all(value_act, 'cam', split_axis=1, concat_axis=0, tiled=True)  24 us
    all_to_all x1, blocking collectives, local(): lax.all_to_all(key_act, 'cam', split_axis=1, concat_axis=0, tiled=True)  22 us
    all_to_all x1, waiting for transfers between devices, local(): lax.all_to_all(grad_value, 'cam', split_axis=0, concat_axis=1, tiled=True)  18.6 us
    all_to_all x1, waiting for transfers between devices, local(): lax.all_to_all(grad_key, 'cam', split_axis=0, concat_axis=1, tiled=True)  16.9 us
    all_to_all x1, waiting for transfers between devices, local(): lax.all_to_all(grad_query, 'cam', split_axis=0, concat_axis=1, tiled=True)  14.1 us
  transfers between devices with their start and end apart: 9, of which 8 were waited for; matrix products, arithmetic and copies ran while one was open for 7% of the time, Pallas kernels for 0%

profile of v1, /device:TPU:1, one launch (start us, length us, event | category | flops | bytes accessed | tf_op | source)
XLA Modules:
  0.0 595.3 jit_solution(14426092489382381939)
XLA Ops:
  9.1 10.0 %all-to-all-start = ((bf16[128,8,256]{2,0,1:T(8,128)(2,1)}), bf16[128,8,256]{2,0,1:T(8,128)(2,1)S(1)}, u32[]{:S(2)}, u32[]{:S(2)}) async-start(bf16[128,8,256]{2,0,1:T(8,128)(2,1)} %bitcast.87), calls=%async_computation | async-start | bytes 1048576 | tf_op jit(solution)/shard_map/all_to_all | solution.py:85
  20.1 13.1 %all-to-all-done = bf16[128,8,256]{2,0,1:T(8,128)(2,1)S(1)} async-done(((bf16[128,8,256]{2,0,1:T(8,128)(2,1)}), bf16[128,8,256]{2,0,1:T(8,128)(2,1)S(1)}, u32[]{:S(2)}, u32[]{:S(2)}) %all-to-all-start) | async-done | bytes 524320 | tf_op jit(solution)/shard_map/all_to_all | solution.py:85
  33.2 22.0 %all_to_all.138 = bf16[128,8,256]{2,0,1:T(8,128)(2,1)S(1)} all-to-all(bf16[128,8,256]{2,0,1:T(8,128)(2,1)S(1)} %bitcast.112), channel_id=1, replica_groups=mesh['dp'=32,'cam'=8] {'cam'}, dimensions={1} | all-to-all | bytes 1048576 | tf_op jit(solution)/shard_map/all_to_all | solution.py:86
  55.2 6.1 %stack.2 = bf16[32,96,2048]{2,1,0:T(8,128)(2,1)} broadcast(bf16[96,2048]{1,0:T(8,128)(2,1)S(1)} %copy-done.8), dimensions={1,2} | broadcast | bytes 12976128 | tf_op jit(solution)/shard_map/stack | solution.py:79
  61.3 7.3 %all-to-all-start.3 = ((bf16[32,96,2048]{2,1,0:T(8,128)(2,1)}), bf16[32,96,2048]{2,1,0:T(8,128)(2,1)}, u32[]{:S(2)}, u32[]{:S(2)}) async-start(bf16[32,96,2048]{2,1,0:T(8,128)(2,1)} %stack.2), calls=%async_computation.3 | async-start | bytes 25165824 | tf_op jit(solution)/shard_map/all_to_all | solution.py:79
  70.1 199.0 %all-to-all-done.3 = bf16[32,96,2048]{2,1,0:T(8,128)(2,1)} async-done(((bf16[32,96,2048]{2,1,0:T(8,128)(2,1)}), bf16[32,96,2048]{2,1,0:T(8,128)(2,1)}, u32[]{:S(2)}, u32[]{:S(2)}) %all-to-all-start.3) | async-done | bytes 12582944 | tf_op jit(solution)/shard_map/all_to_all | solution.py:79
  269.1 24.0 %all-to-all-start.2 = ((bf16[128,8,256]{2,0,1:T(8,128)(2,1)}), bf16[128,8,256]{2,0,1:T(8,128)(2,1)S(1)}, u32[]{:S(2)}, u32[]{:S(2)}) async-start(bf16[128,8,256]{2,0,1:T(8,128)(2,1)} %bitcast.85), calls=%async_computation.2 | async-start | bytes 1048576 | tf_op jit(solution)/shard_map/all_to_all | solution.py:87
  293.1 6.4 %convolution_convert_fusion.1 = bf16[128,2048]{1,0:T(8,128)(2,1)S(1)} fusion(bf16[128,3072]{1,0:T(8,128)(2,1)S(1)} %copy-done.2, bf16[3072,2048]{1,0:T(8,128)(2,1)} %bitcast.6), kind=kOutput, calls=%fused_computation.37 | convolution fusion | flops 1610874880 | bytes 13893632 | tf_op jit(solution)/shard_map/dot_general | solution.py:81
  300.4 8.1 %all-to-all-done.2 = bf16[128,8,256]{2,0,1:T(8,128)(2,1)S(1)} async-done(((bf16[128,8,256]{2,0,1:T(8,128)(2,1)}), bf16[128,8,256]{2,0,1:T(8,128)(2,1)S(1)}, u32[]{:S(2)}, u32[]{:S(2)}) %all-to-all-start.2) | async-done | bytes 524320 | tf_op jit(solution)/shard_map/all_to_all | solution.py:87
  308.5 4.1 all-to-all-start.4
  313.1 12.9 %all-to-all-done.4 = bf16[128,8,256]{2,0,1:T(8,128)(2,1)S(1)} async-done(((bf16[128,8,256]{2,0,1:T(8,128)(2,1)}), bf16[128,8,256]{2,0,1:T(8,128)(2,1)S(1)}, u32[]{:S(2)}, u32[]{:S(2)}) %all-to-all-start.4) | async-done | bytes 524320 | tf_op jit(solution)/shard_map/all_to_all | solution.py:88
  326.0 29.8 %while.17 = (s32[]{:T(128)}, bf16[2,1024,128]{1,2,0:T(8,128)(2,1)}, bf16[2,1024,128]{2,1,0:T(8,128)(2,1)}, bf16[2,1024,128]{2,1,0:T(8,128)(2,1)S(1)}, bf16[2,102...) while((s32[]{:T(128)}, bf16[2,1024,128]{1,2,0:T(8,128)(2,1)}, ...), condition=%wide.region_7.8_spmd.clone, body=%wide.region_3.7_spmd.clone.sunk | while | flops 1631712256 | bytes 83147144 | solution.py:65
  334.1 3.0 multiply_convert_fusion.2
  349.0 3.0 multiply_convert_fusion.2
  356.6 4.8 convolution_bitcast_fusion
  361.3 2.3 copy.89
  366.0 8.4 %all-to-all-start.5 = ((bf16[8,128,256]{1,2,0:T(8,128)(2,1)}), bf16[8,128,256]{1,2,0:T(8,128)(2,1)S(1)}, u32[]{:S(2)}, u32[]{:S(2)}) async-start(bf16[8,128,256]{1,2,0:T(8,128)(2,1)} %copy.79), calls=%async_computation.5 | async-start | bytes 1048576 | tf_op jit(solution)/shard_map/all_to_all | solution.py:104
  375.6 14.1 %all-to-all-done.5 = bf16[8,128,256]{1,2,0:T(8,128)(2,1)S(1)} async-done(((bf16[8,128,256]{1,2,0:T(8,128)(2,1)}), bf16[8,128,256]{1,2,0:T(8,128)(2,1)S(1)}, u32[]{:S(2)}, u32[]{:S(2)}) %all-to-all-start.5) | async-done | bytes 524320 | tf_op jit(solution)/shard_map/all_to_all | solution.py:104
  389.7 5.8 all-to-all-start.6
  397.8 16.9 %all-to-all-done.6 = bf16[8,128,256]{1,2,0:T(8,128)(2,1)S(1)} async-done(((bf16[8,128,256]{1,2,0:T(8,128)(2,1)}), bf16[8,128,256]{1,2,0:T(8,128)(2,1)S(1)}, u32[]{:S(2)}, u32[]{:S(2)}) %all-to-all-start.6) | async-done | bytes 524320 | tf_op jit(solution)/shard_map/all_to_all | solution.py:105
  414.6 4.8 all-to-all-start.7
  421.4 18.6 %all-to-all-done.7 = bf16[8,128,256]{1,2,0:T(8,128)(2,1)S(1)} async-done(((bf16[8,128,256]{1,2,0:T(8,128)(2,1)}), bf16[8,128,256]{1,2,0:T(8,128)(2,1)S(1)}, u32[]{:S(2)}, u32[]{:S(2)}) %all-to-all-start.7) | async-done | bytes 524320 | tf_op jit(solution)/shard_map/all_to_all | solution.py:106
  441.1 105.9 %reduce-scatter.4.cloned.1.call-done = f32[96,256]{1,0:T(8,128)} async-done(((f32[3072,256]{1,0:T(8,128)}), f32[96,256]{1,0:T(8,128)}) %reduce-scatter.4.cloned.1.call-update) | async-done | bytes 98320
  547.9 39.3 %all_gather.7 = f32[96,2048]{0,1:T(8,128)S(1)} all-gather(f32[96,256]{0,1:T(8,128)S(1)} %copy.90), channel_id=1, replica_groups=mesh['dp'=32,'cam'=8] {'cam'}, dimensions={1}, use_global_device_ids=true | all-gather | bytes 884736 | tf_op jit(solution)/shard_map/all_gather | solution.py:102
  (93 shorter events, 39.9 us)
Async XLA Ops:
  7.2 48.0 %copy-start.8 = (bf16[96,2048]{1,0:T(8,128)(2,1)S(1)}, bf16[96,2048]{1,0:T(8,128)(2,1)}, u32[]{:S(2)}) copy-start(bf16[96,2048]{1,0:T(8,128)(2,1)} %param.13) | copy-start | bytes 1179652
  9.1 24.1 %all-to-all-start = ((bf16[128,8,256]{2,0,1:T(8,128)(2,1)}), bf16[128,8,256]{2,0,1:T(8,128)(2,1)S(1)}, u32[]{:S(2)}, u32[]{:S(2)}) async-start(bf16[128,8,256]{2,0,1:T(8,128)(2,1)} %bitcast.87), calls=%async_computation | async-start | bytes 1048576 | tf_op jit(solution)/shard_map/all_to_all | solution.py:85
  61.3 8.0 %copy-start.3 = (bf16[128,2048]{1,0:T(8,128)(2,1)S(1)}, bf16[128,2048]{1,0:T(8,128)(2,1)}, u32[]{:S(2)}) copy-start(bf16[128,2048]{1,0:T(8,128)(2,1)} %param.12) | copy-start | bytes 1572868
  61.3 231.9 %copy-start.2 = (bf16[128,3072]{1,0:T(8,128)(2,1)S(1)}, bf16[128,3072]{1,0:T(8,128)(2,1)}, u32[]{:S(2)}) copy-start(bf16[128,3072]{1,0:T(8,128)(2,1)} %param.9) | copy-start | bytes 2359300
  61.3 207.8 %all-to-all-start.3 = ((bf16[32,96,2048]{2,1,0:T(8,128)(2,1)}), bf16[32,96,2048]{2,1,0:T(8,128)(2,1)}, u32[]{:S(2)}, u32[]{:S(2)}) async-start(bf16[32,96,2048]{2,1,0:T(8,128)(2,1)} %stack.2), calls=%async_computation.3 | async-start | bytes 25165824 | tf_op jit(solution)/shard_map/all_to_all | solution.py:79
  68.6 287.2 %all-gather.2.cloned.1.call-start = ((), (), s32[]{:S(2)}) async-start(), calls=%async_computation.9 | async-start | bytes 7077888 | tf_op jit(solution)/shard_map/all_gather | solution.py:76
  269.1 39.4 %all-to-all-start.2 = ((bf16[128,8,256]{2,0,1:T(8,128)(2,1)}), bf16[128,8,256]{2,0,1:T(8,128)(2,1)S(1)}, u32[]{:S(2)}, u32[]{:S(2)}) async-start(bf16[128,8,256]{2,0,1:T(8,128)(2,1)} %bitcast.85), calls=%async_computation.2 | async-start | bytes 1048576 | tf_op jit(solution)/shard_map/all_to_all | solution.py:87
  293.1 19.5 %copy-start.11 = (s32[1,4]{1,0:T(1,128)S(1)}, s32[1,4]{1,0:T(1,128)}, u32[]{:S(2)}) copy-start(s32[1,4]{1,0:T(1,128)} %param.14) | copy-start | bytes 52
  293.1 19.8 %copy-start.12 = (s32[1,16]{1,0:T(1,128)S(1)}, s32[1,16]{1,0:T(1,128)}, u32[]{:S(2)}) copy-start(s32[1,16]{1,0:T(1,128)} %param.15) | copy-start | bytes 196
  308.5 17.5 %all-to-all-start.4 = ((bf16[128,8,256]{2,0,1:T(8,128)(2,1)}), bf16[128,8,256]{2,0,1:T(8,128)(2,1)S(1)}, u32[]{:S(2)}, u32[]{:S(2)}) async-start(bf16[128,8,256]{2,0,1:T(8,128)(2,1)} %bitcast.84), calls=%async_computation.4 | async-start | bytes 1048576 | tf_op jit(solution)/shard_map/all_to_all | solution.py:88
  312.6 234.3 %reduce-scatter.4.cloned.1.call-start = ((), (), s32[]{:S(2)}) async-start(), calls=%async_computation.10 | async-start | bytes 3244032
  326.0 3.1 copy-start.4
  329.2 3.4 copy-start.9
  330.6 2.0 copy-start
  334.1 3.8 copy-start.5
  337.1 2.4 copy-start.1
  340.9 3.1 copy-start.4
  344.0 3.4 copy-start.9
  349.0 3.9 copy-start.5
  352.0 2.4 copy-start.1
  363.7 10.7 %copy-start.7 = (bf16[2,1024,128]{2,1,0:T(8,128)(2,1)S(1)}, bf16[2,1024,128]{2,1,0:T(8,128)(2,1)}, u32[]{:S(2)}) copy-start(bf16[2,1024,128]{2,1,0:T(8,128)(2,1)} %copy-done.6) | copy-start | bytes 1572868
  366.0 23.7 %all-to-all-start.5 = ((bf16[8,128,256]{1,2,0:T(8,128)(2,1)}), bf16[8,128,256]{1,2,0:T(8,128)(2,1)S(1)}, u32[]{:S(2)}, u32[]{:S(2)}) async-start(bf16[8,128,256]{1,2,0:T(8,128)(2,1)} %copy.79), calls=%async_computation.5 | async-start | bytes 1048576 | tf_op jit(solution)/shard_map/all_to_all | solution.py:104
  389.7 24.9 %all-to-all-start.6 = ((bf16[8,128,256]{1,2,0:T(8,128)(2,1)}), bf16[8,128,256]{1,2,0:T(8,128)(2,1)S(1)}, u32[]{:S(2)}, u32[]{:S(2)}) async-start(bf16[8,128,256]{1,2,0:T(8,128)(2,1)} %copy.81), calls=%async_computation.6 | async-start | bytes 1048576 | tf_op jit(solution)/shard_map/all_to_all | solution.py:105
  414.6 25.4 %all-to-all-start.7 = ((bf16[8,128,256]{1,2,0:T(8,128)(2,1)}), bf16[8,128,256]{1,2,0:T(8,128)(2,1)S(1)}, u32[]{:S(2)}, u32[]{:S(2)}) async-start(bf16[8,128,256]{1,2,0:T(8,128)(2,1)} %copy.83), calls=%async_computation.7 | async-start | bytes 1048576 | tf_op jit(solution)/shard_map/all_to_all | solution.py:106
  (4 other events, 4.3 us)
Sparse Core Ops, SparseCore 0:
  71.2 95.8 all-gather.1
  363.8 183.0 reduce-scatter.3
